TPU v7x, 32 devices: a whole 2x2x4 slice. The times are simulated.
32 devices in a mesh: dp: 8 (over y, x, core), context: 4 (over z).
Axes of the slice: x: 2, y: 2, z: 4, core: 2. Of those that a mesh axis runs over, the one named last changes fastest.
Arguments:
- image_tokens: bfloat16 [8, 448, 3072], P('dp', 'context'), may hold values from -6 to 6
- text_tokens: bfloat16 [8, 64, 3072], P('dp', 'context'), may hold values from -6 to 6
- image_mod: bfloat16 [8, 3, 3072], P('dp'), may hold values from -4 to 4
- text_mod: bfloat16 [8, 3, 3072], P('dp'), may hold values from -4 to 4
- image_qkv_weight: bfloat16 [3072, 3, 16, 128], P('dp', None, 'context'), may hold values from -0.109375 to 0.109375
- text_qkv_weight: bfloat16 [3072, 3, 16, 128], P('dp', None, 'context'), may hold values from -0.109375 to 0.109375
- image_out_weight: bfloat16 [3072, 16, 128], P('dp', 'context'), may hold values from -1 to 1
- text_out_weight: bfloat16 [3072, 16, 128], P('dp', 'context'), may hold values from -1 to 1
- image_slope: bfloat16 [8, 448, 3072], P('dp', 'context'), may hold values from -0.119628906 to 0.119628906
- text_slope: bfloat16 [8, 64, 3072], P('dp', 'context'), may hold values from -0.119628906 to 0.119628906
Outputs:
- image_update: bfloat16 [8, 448, 3072], P('dp', 'context')
- text_update: bfloat16 [8, 64, 3072], P('dp', 'context')
- image_qkv_grad: float32 [3072, 3, 16, 128], P('dp', None, 'context')
- text_qkv_grad: float32 [3072, 3, 16, 128], P('dp', None, 'context')
- image_out_grad: float32 [3072, 16, 128], P('dp', 'context')
- text_out_grad: float32 [3072, 16, 128], P('dp', 'context')
- image_mod_grad: float32 [8, 3, 3072], P('dp')
- text_mod_grad: float32 [8, 3, 3072], P('dp')
All inputs are finite; a program needn't handle non-finite values.
Results may differ from a plain program's by a relative error of at most 0.015.
Values may be sent and summed in bfloat16 or wider, within the bound.
No kernel may reach another device: no remote copies, remote signals or barrier semaphores. Data moves between devices by JAX's collectives and lax.ppermute only.
A program may use at most 128 MiB of HBM per device.

v0:
```python
import jax
import jax.numpy as jnp
from jax import lax
from jax.sharding import PartitionSpec as P

norm_eps = 1e-06


def layer_normal(values):
    average = jnp.mean(values, axis=-1, keepdims=True)
    centred = values - average
    return centred * lax.rsqrt(jnp.mean(centred * centred, axis=-1, keepdims=True) + norm_eps)


def rms_normal(values):
    factor = lax.rsqrt(jnp.mean(values * values, axis=-1, keepdims=True) + norm_eps)
    return (values * factor, factor)


def rms_back(normed, factor, slopes):
    return factor * (slopes - normed * jnp.mean(slopes * normed, axis=-1, keepdims=True))


def modulate(tokens, modulation):
    normal = layer_normal(tokens.astype(jnp.float32))
    factors = modulation.astype(jnp.float32)
    return (normal, ((1.0 + factors[1]) * normal + factors[0]).astype(jnp.bfloat16))


def contract_rows(left_side, right_side):
    return lax.dot_general(
        left_side, right_side, (((0,), (0,)), ((), ())), preferred_element_type=jnp.float32
    )


def contract_last(left_side, right_side):
    return lax.dot_general(
        left_side, right_side, (((1,), (1,)), ((), ())), preferred_element_type=jnp.float32
    )


def body(
    image_tokens,
    text_tokens,
    image_mod,
    text_mod,
    image_qkv_weight,
    text_qkv_weight,
    image_out_weight,
    text_out_weight,
    image_slope,
    text_slope,
):
    groups = lax.axis_size("context")
    own_image = image_tokens.shape[1]
    own_text = text_tokens.shape[1]
    block_rows = own_image + own_text
    model_width = image_tokens.shape[2]
    shard_rows = image_qkv_weight.shape[0]
    head_count = image_qkv_weight.shape[2]
    head_size = image_qkv_weight.shape[3]
    inner_width = head_count * head_size
    triple = 3 * inner_width
    text_rows = own_text * groups
    score_scale = head_size ** (-0.5)
    whole_image, whole_text, slopes_image, slopes_text = (
        lax.all_gather(image_tokens, "context", axis=1, tiled=True),
        lax.all_gather(text_tokens, "context", axis=1, tiled=True),
        lax.all_gather(image_slope, "context", axis=1, tiled=True),
        lax.all_gather(text_slope, "context", axis=1, tiled=True),
    )
    full_q_image, full_q_text, full_o_image, full_o_text = (
        lax.all_gather(image_qkv_weight, "dp", axis=0, tiled=True),
        lax.all_gather(text_qkv_weight, "dp", axis=0, tiled=True),
        lax.all_gather(image_out_weight, "dp", axis=0, tiled=True),
        lax.all_gather(text_out_weight, "dp", axis=0, tiled=True),
    )
    wq_image = full_q_image.reshape(model_width, triple)
    wq_text = full_q_text.reshape(model_width, triple)
    wo_image = full_o_image.reshape(model_width, inner_width)
    wo_text = full_o_text.reshape(model_width, inner_width)
    normal_image, input_image = modulate(whole_image[0], image_mod[0])
    normal_text, input_text = modulate(whole_text[0], text_mod[0])
    projected = jnp.concatenate(
        [
            jnp.dot(input_text, wq_text, preferred_element_type=jnp.float32),
            jnp.dot(input_image, wq_image, preferred_element_type=jnp.float32),
        ],
        axis=0,
    )
    projected = projected.reshape(-1, 3, head_count, head_size)
    query_normal, query_factor = rms_normal(projected[:, 0])
    key_normal, key_factor = rms_normal(projected[:, 1])
    query_b = query_normal.astype(jnp.bfloat16)
    key_b = key_normal.astype(jnp.bfloat16)
    value_b = projected[:, 2].astype(jnp.bfloat16)
    scores = (
        jnp.einsum("ihe,jhe->hij", query_b, key_b, preferred_element_type=jnp.float32) * score_scale
    )
    raised = jnp.exp(scores)
    attn_probs = raised / jnp.sum(raised, axis=-1, keepdims=True)
    probs_b = attn_probs.astype(jnp.bfloat16)
    attended = jnp.einsum(
        "hij,jhe->ihe", probs_b, value_b, preferred_element_type=jnp.float32
    ).astype(jnp.bfloat16)
    flat_att = attended.reshape(-1, inner_width)
    att_text = flat_att[:text_rows]
    att_image = flat_att[text_rows:]
    blocks_text = att_text.reshape(groups, own_text, inner_width)
    blocks_image = att_image.reshape(groups, own_image, inner_width)
    block_count = block_rows * lax.axis_size("context") // block_rows
    part_text = blocks_text.reshape(block_count * own_text, inner_width)
    part_image = blocks_image.reshape(block_count * own_image, inner_width)
    out_text = contract_last(part_text, wo_text).reshape(block_count, own_text, model_width)
    out_image = contract_last(part_image, wo_image).reshape(block_count, own_image, model_width)
    mixed_rows = lax.psum_scatter(
        jnp.concatenate([out_text, out_image], axis=1)
        .reshape(block_rows * lax.axis_size("context"), model_width)
        .astype(jnp.bfloat16),
        "context",
        scatter_dimension=0,
        tiled=True,
    ).astype(jnp.float32)
    mixed_text = mixed_rows[:own_text]
    mixed_image = mixed_rows[own_text:]
    factors_image = image_mod[0].astype(jnp.float32)
    factors_text = text_mod[0].astype(jnp.float32)
    update_image = (factors_image[2] * mixed_image).astype(jnp.bfloat16)[None]
    update_text = (factors_text[2] * mixed_text).astype(jnp.bfloat16)[None]
    gate_part_image = jnp.sum(image_slope[0].astype(jnp.float32) * mixed_image, axis=0)
    gate_part_text = jnp.sum(text_slope[0].astype(jnp.float32) * mixed_text, axis=0)
    gated_image = (factors_image[2] * slopes_image[0].astype(jnp.float32)).astype(jnp.bfloat16)
    gated_text = (factors_text[2] * slopes_text[0].astype(jnp.float32)).astype(jnp.bfloat16)
    back_att = jnp.concatenate(
        [
            jnp.dot(gated_text, wo_text, preferred_element_type=jnp.float32),
            jnp.dot(gated_image, wo_image, preferred_element_type=jnp.float32),
        ],
        axis=0,
    )
    back_att = back_att.astype(jnp.bfloat16).reshape(-1, head_count, head_size)
    back_probs = jnp.einsum("ihe,jhe->hij", back_att, value_b, preferred_element_type=jnp.float32)
    back_value = jnp.einsum("hij,ihe->jhe", probs_b, back_att, preferred_element_type=jnp.float32)
    back_scores = (
        attn_probs
        * (back_probs - jnp.sum(attn_probs * back_probs, axis=-1, keepdims=True))
        * score_scale
    ).astype(jnp.bfloat16)
    back_query = jnp.einsum("hij,jhe->ihe", back_scores, key_b, preferred_element_type=jnp.float32)
    back_key = jnp.einsum("hij,ihe->jhe", back_scores, query_b, preferred_element_type=jnp.float32)
    back_qkv = (
        jnp.stack(
            [
                rms_back(query_normal, query_factor, back_query),
                rms_back(key_normal, key_factor, back_key),
                back_value,
            ],
            axis=1,
        )
        .reshape(-1, triple)
        .astype(jnp.bfloat16)
    )
    back_text = back_qkv[:text_rows]
    back_image = back_qkv[text_rows:]
    spread_image = contract_last(back_image, wq_image)
    spread_text = contract_last(back_text, wq_text)
    part_image = jnp.stack(
        [
            jnp.sum(spread_image, axis=0),
            jnp.sum(spread_image * normal_image, axis=0),
            gate_part_image,
        ]
    )
    part_text = jnp.stack(
        [jnp.sum(spread_text, axis=0), jnp.sum(spread_text * normal_text, axis=0), gate_part_text]
    )
    modsum_image, modsum_text = (
        lax.psum(part_image.astype(jnp.bfloat16), "context").astype(jnp.float32),
        lax.psum(part_text.astype(jnp.bfloat16), "context").astype(jnp.float32),
    )
    pieces = [contract_rows(input_image, back_image)]
    pieces.append(contract_rows(gated_image, att_image))
    pieces.append(contract_rows(gated_text, att_text))
    summed = lax.psum_scatter(
        jnp.concatenate(pieces, axis=1).astype(jnp.bfloat16), "dp", scatter_dimension=0, tiled=True
    ).astype(jnp.float32)
    grad_q_image = summed[:, :triple]
    remaining = summed[:, triple:]
    columns = lax.all_to_all(input_text[None], "dp", split_axis=2, concat_axis=0, tiled=True)
    slopes_all = lax.all_gather(back_text[None], "dp", axis=0, tiled=True)
    per_image = jnp.einsum("itd,itj->idj", columns, slopes_all, preferred_element_type=jnp.float32)
    rounded = lax.optimization_barrier(per_image.astype(jnp.bfloat16))
    grad_q_text = jnp.sum(rounded.astype(jnp.float32), axis=0)
    grad_o_image = remaining[:, :inner_width]
    grad_o_text = remaining[:, inner_width:]
    return (
        update_image,
        update_text,
        grad_q_image.reshape(shard_rows, 3, head_count, head_size),
        grad_q_text.reshape(shard_rows, 3, head_count, head_size),
        grad_o_image.reshape(shard_rows, head_count, head_size),
        grad_o_text.reshape(shard_rows, head_count, head_size),
        modsum_image[None],
        modsum_text[None],
    )


def solution(mesh):
    placed = (
        P("dp", "context", None),
        P("dp", "context", None),
        P("dp", None, None),
        P("dp", None, None),
        P("dp", None, "context", None),
        P("dp", None, "context", None),
        P("dp", "context", None),
        P("dp", "context", None),
        P("dp", "context", None),
        P("dp", "context", None),
    )
    return jax.shard_map(
        body,
        mesh=mesh,
        in_specs=placed,
        out_specs=(
            P("dp", "context", None),
            P("dp", "context", None),
            P("dp", None, "context", None),
            P("dp", None, "context", None),
            P("dp", "context", None),
            P("dp", "context", None),
            P("dp", None, None),
            P("dp", None, None),
        ),
        check_vma=False,
    )
```

profile of v0, /device:TPU:0, one launch (start us, length us, event | category | flops | bytes accessed | tf_op | source)
XLA Modules:
  0.0 606.1 jit_solution(18341433870807146927)
XLA Ops:
  11.3 19.2 %all_gather.27 = bf16[1,64,3072]{2,1,0:T(8,128)(2,1)S(1)} all-gather(bf16[1,16,3072]{2,1,0:T(8,128)(2,1)S(1)} %copy-done.28), channel_id=1, replica_groups=mesh['dp'=8,'context'=4] {'context'}, dimensions={1}, use_global_device_ids=true | all-gather | bytes 491520 | tf_op jit(solution)/shard_map/all_gather | solution.py:68
  30.9 19.6 %all_gather.33 = bf16[1,64,3072]{2,1,0:T(8,128)(2,1)} all-gather(bf16[1,16,3072]{2,1,0:T(8,128)(2,1)S(1)} %copy-done.23), channel_id=1, replica_groups=mesh['dp'=8,'context'=4] {'context'}, dimensions={1}, use_global_device_ids=true | all-gather | bytes 491520 | tf_op jit(solution)/shard_map/all_gather | solution.py:70
  52.8 24.9 %all-gather.10.cloned.1.call-done = bf16[1,448,3072]{2,1,0:T(8,128)(2,1)} async-done(((bf16[1,112,3072]{2,1,0:T(8,128)(2,1)}), bf16[1,448,3072]{2,1,0:T(8,128)(2,1)}) %all-gather.10.cloned.1.call-update) | async-done | bytes 2752528 | tf_op jit(solution)/shard_map/all_gather | solution.py:67
  81.7 29.0 %all-gather.14.cloned.1.call-done = bf16[3072,4,128]{2,1,0:T(4,128)(2,1)} async-done(((bf16[384,4,128]{2,1,0:T(4,128)(2,1)}), bf16[3072,4,128]{2,1,0:T(4,128)(2,1)}) %all-gather.14.cloned.1.call-update) | async-done | bytes 3145744 | tf_op jit(solution)/shard_map/all_gather | solution.py:76
  110.7 4.1 copy.103
  118.2 26.6 %all-gather.16.cloned.1.call-done = bf16[3072,4,128]{2,1,0:T(4,128)(2,1)} async-done(((bf16[384,4,128]{2,1,0:T(4,128)(2,1)}), bf16[3072,4,128]{2,1,0:T(4,128)(2,1)}) %all-gather.16.cloned.1.call-update) | async-done | bytes 3145744 | tf_op jit(solution)/shard_map/all_gather | solution.py:75
  144.8 4.1 copy.102
  149.0 4.6 copy.89
  156.3 46.9 %all-gather.18.cloned.1.call-done = bf16[1,448,3072]{2,1,0:T(8,128)(2,1)} async-done(((bf16[1,112,3072]{2,1,0:T(8,128)(2,1)}), bf16[1,448,3072]{2,1,0:T(8,128)(2,1)}) %all-gather.18.cloned.1.call-update) | async-done | bytes 2752528 | tf_op jit(solution)/shard_map/all_gather | solution.py:69
  203.2 5.1 fusion.49
  208.3 54.1 %all-gather.8.cloned.1.call-done = bf16[3072,3,4,128]{3,2,1,0:T(4,128)(2,1)} async-done(((bf16[384,3,4,128]{3,2,1,0:T(4,128)(2,1)}), bf16[3072,3,4,128]{3,2,1,0:T(4,128)(2,1)}) %all-gather.8.cloned.1.call-update) | async-done | bytes 9437200 | tf_op jit(solution)/shard_map/all_gather | solution.py:74
  262.4 16.2 %reshape.247 = bf16[3072,1536]{1,0:T(8,128)(2,1)} reshape(bf16[3072,3,4,128]{3,2,1,0:T(4,128)(2,1)} %all-gather.8.cloned.1.call-done) | data formatting | bytes 18874368 | tf_op jit(solution)/shard_map/reshape | solution.py:79
  278.6 5.4 fusion.78
  284.0 38.9 %all-gather.12.cloned.1.call-done = bf16[3072,3,4,128]{3,2,1,0:T(4,128)(2,1)} async-done(((bf16[384,3,4,128]{3,2,1,0:T(4,128)(2,1)}), bf16[3072,3,4,128]{3,2,1,0:T(4,128)(2,1)}) %all-gather.12.cloned.1.call-update) | async-done | bytes 9437200 | tf_op jit(solution)/shard_map/all_gather | solution.py:73
  322.9 15.9 %reshape.248 = bf16[3072,1536]{1,0:T(8,128)(2,1)} reshape(bf16[3072,3,4,128]{3,2,1,0:T(4,128)(2,1)} %all-gather.12.cloned.1.call-done) | data formatting | bytes 18874368 | tf_op jit(solution)/shard_map/reshape | solution.py:78
  338.8 7.6 %fusion.21 = f32[448,1536]{1,0:T(8,128)S(1)} fusion(bf16[3072,1536]{1,0:T(8,128)(2,1)} %reshape.248, bf16[1,448,3072]{2,1,0:T(8,128)(2,1)S(1)} %copy-done.1, f32[3072]{0:T(1024)} %bitcast.215, f32[448]{0:T(512)} %add_rsqrt_fusion.2, f32[448]{0:T(512)S(1)} %broadcast_multiply_fusion.2, f32[3072]{0:T(1024)} %bitcast.213), kind=kOutput, calls=%fused_computation.37 | convolution fusion | flops 4236115968 | bytes 14970368 | tf_op jit(solution)/shard_map/dot_general | solution.py:87
  351.0 3.7 fusion.80
  359.4 8.2 %fusion.46 = f32[512,4,128]{0,2,1:T(8,128)} fusion(f32[4,512,512]{1,2,0:T(8,128)} %fusion.80, f32[512,3,4,128]{0,3,2,1:T(8,128)S(1)} %bitcast.182, f32[512,4]{0,1:T(4,128)} %copy-done.30, f32[4,512,512]{1,2,0:T(8,128)} %copy-done.10, f32[4,512]{1,0:T(4,128)} %copy-done.35), kind=kOutput, calls=%fused_computation.58 | convolution fusion | flops 278399488 | bytes 18898944 | tf_op jit(solution)/shard_map/hij,ihe->jhe/dot_general | solution.py:150
  367.6 10.0 %multiply_reduce_fusion.2 = (f32[512,4]{0,1:T(4,128)}, f32[512,4]{0,1:T(4,128)}, f32[512,4,128]{0,2,1:T(8,128)}) fusion(f32[512,3,4,128]{0,3,2,1:T(8,128)S(1)} %bitcast.183, f32[512,4]{0,1:T(4,128)} %copy-done.30, f32[512,4,128]{0,2,1:T(8,128)} %fusion.46, f32[512,4]{0,1:T(4,128)} %copy-done.29, f32[4,512,512]{1,2,0:T(8,128)} %fusion.80, ...), kind=kOutput, calls=%fused_computation.74 | convolution fusion | flops 279968256 | bytes 22077440 | tf_op jit(solution)/shard_map/hij,jhe->ihe/dot_general | solution.py:149
  384.6 5.7 reshape.258
  390.3 5.8 reshape.259
  418.7 6.2 %convolution_convert_fusion = bf16[3072,1536]{0,1:T(8,128)(2,1)S(1)} fusion(bf16[448,1536]{0,1:T(8,128)(2,1)S(1)} %bitcast.202, bf16[1,448,3072]{2,1,0:T(8,128)(2,1)S(1)} %copy-done.2, f32[3072]{0:T(1024)S(1)} %bitcast.216, f32[448]{0:T(512)S(1)} %copy-done.38, f32[3072]{0:T(1024)S(1)} %bitcast.214, f32[448]{0:T(512)S(1)} %broadcast_multiply_fusion.2), kind=kOutput, calls=%fused_computation.3 | convolution fusion | flops 4240834560 | bytes 13594112 | tf_op jit(solution)/shard_map/dot_general | solution.py:31
  424.9 7.6 %pad_maximum_fusion = bf16[3072,2560]{0,1:T(8,128)(2,1)} fusion(bf16[3072,512]{0,1:T(8,128)(2,1)S(1)} %convolution_convert_fusion.2, bf16[3072,512]{0,1:T(8,128)(2,1)S(1)} %convolution_convert_fusion.3, bf16[3072,1536]{0,1:T(8,128)(2,1)S(1)} %convolution_convert_fusion), kind=kLoop, calls=%fused_computation.2 | loop fusion | flops 47185920 | bytes 31457280 | tf_op jit(solution)/shard_map/concatenate | solution.py:185
  432.5 20.1 %copy.92 = bf16[3072,2560]{1,0:T(8,128)(2,1)} copy(bf16[3072,2560]{0,1:T(8,128)(2,1)} %pad_maximum_fusion) | data formatting | bytes 31457280
  457.0 18.9 %reduce.2 = bf16[3072,64]{1,0:T(8,128)(2,1)} reduce(bf16[3072,1,64]{2,1,0:T(2,128)(2,1)} %bitcast.193, bf16[]{:T(256)} %broadcast.209), dimensions={1}, to_apply=%bitcast.152.reduce_sub_computation | reduce | bytes 786434
  478.6 12.6 %all_to_all.18 = bf16[8,2,12288]{2,1,0:T(2,128)(2,1)} all-to-all(bf16[8,2,12288]{2,1,0:T(2,128)(2,1)} %reshape.268), channel_id=1, replica_groups=mesh['dp'=8,'context'=4] {'dp'}, dimensions={0} | all-to-all | bytes 786432 | tf_op jit(solution)/shard_map/all_to_all | solution.py:189
  491.2 3.7 reshape.269
  500.1 7.3 %fusion.103 = (bf16[3072]{0:T(1024)(128)(2,1)S(1)}, bf16[3072]{0:T(1024)(128)(2,1)S(1)}) fusion(f32[64]{0:T(128)} %copy-done.37, f32[64]{0:T(128)} %copy-done.36, bf16[1,64,3072]{2,1,0:T(8,128)(2,1)S(1)} %all_gather.27, bf16[64,1536]{0,1:T(8,128)(2,1)S(1)} %bitcast.196, bf16[3072,1536]{1,0:T(8,128)(2,1)} %reshape.247), kind=kOutput, calls=%fused_computation.131 | convolution fusion | flops 605153280 | bytes 10039808 | tf_op jit(solution)/shard_map/dot_general | solution.py:37
  507.5 9.5 %fusion.102 = (bf16[3072]{0:T(1024)(128)(2,1)S(1)}, bf16[3072]{0:T(1024)(128)(2,1)S(1)}) fusion(f32[448]{0:T(512)S(1)} %copy-done.39, f32[448]{0:T(512)S(1)} %broadcast_multiply_fusion.2, bf16[1,448,3072]{2,1,0:T(8,128)(2,1)S(1)} %copy-done.2, bf16[448,1536]{0,1:T(8,128)(2,1)S(1)} %bitcast.203, bf16[3072,1536]{1,0:T(8,128)(2,1)} %reshape.248), kind=kOutput, calls=%fused_computation.130 | convolution fusion | flops 4236109824 | bytes 13581824 | tf_op jit(solution)/shard_map/dot_general | solution.py:37
  517.0 4.0 convolution_convert_fusion.1
  527.6 19.2 %all-reduce = (bf16[1,3,3072]{2,0,1:T(2,128)(2,1)S(1)}, bf16[1,3,3072]{2,0,1:T(2,128)(2,1)S(1)}) all-reduce(bf16[1,3,3072]{2,0,1:T(2,128)(2,1)S(1)} %broadcast_in_dim.37, bf16[1,3,3072]{2,0,1:T(2,128)(2,1)S(1)} %broadcast_in_dim.39), channel_id=1, replica_groups=mesh['dp'=8,'context'=4] {'context'}, use_global_device_ids=true, to_apply=%region_16.0 | all-reduce | flops 18432 | bytes 73728 | tf_op jit(solution)/shard_map/psum | solution.py:178
  548.1 39.9 %reduce-scatter.7.cloned.1.call-done = bf16[384,2560]{1,0:T(8,128)(2,1)} async-done(((bf16[3072,2560]{1,0:T(8,128)(2,1)}), bf16[384,2560]{1,0:T(8,128)(2,1)}) %reduce-scatter.7.cloned.1.call-update) | async-done | bytes 1966096
  (171 shorter events, 86.7 us)
Async XLA Ops:
  7.2 4.0 copy-start.26
  7.2 4.1 copy-start.27
  7.2 4.1 copy-start.28
  7.2 23.7 %copy-start.23 = (bf16[1,16,3072]{2,1,0:T(8,128)(2,1)S(1)}, bf16[1,16,3072]{2,1,0:T(8,128)(2,1)}, u32[]{:S(2)}) copy-start(bf16[1,16,3072]{2,1,0:T(8,128)(2,1)} %param.19) | copy-start | bytes 294916
  7.2 70.4 %all-gather.10.cloned.1.call-start = ((), (), s32[]{:S(2)}) async-start(), calls=%async_computation.4 | async-start | bytes 3440640 | tf_op jit(solution)/shard_map/all_gather | solution.py:67
  7.9 102.8 %all-gather.14.cloned.1.call-start = ((), (), s32[]{:S(2)}) async-start(), calls=%async_computation.6 | async-start | bytes 3538944 | tf_op jit(solution)/shard_map/all_gather | solution.py:76
  8.7 136.1 %all-gather.16.cloned.1.call-start = ((), (), s32[]{:S(2)}) async-start(), calls=%async_computation.7 | async-start | bytes 3538944 | tf_op jit(solution)/shard_map/all_gather | solution.py:75
  9.4 193.8 %all-gather.18.cloned.1.call-start = ((), (), s32[]{:S(2)}) async-start(), calls=%async_computation.9 | async-start | bytes 3440640 | tf_op jit(solution)/shard_map/all_gather | solution.py:69
  10.0 252.4 %all-gather.8.cloned.1.call-start = ((), (), s32[]{:S(2)}) async-start(), calls=%async_computation.3 | async-start | bytes 10616832 | tf_op jit(solution)/shard_map/all_gather | solution.py:74
  10.6 312.3 %all-gather.12.cloned.1.call-start = ((), (), s32[]{:S(2)}) async-start(), calls=%async_computation.5 | async-start | bytes 10616832 | tf_op jit(solution)/shard_map/all_gather | solution.py:73
  11.2 505.8 %all-gather.20.cloned.1.call-start = ((), (), s32[]{:S(2)}) async-start(), calls=%async_computation.10 | async-start | bytes 1769472 | tf_op jit(solution)/shard_map/all_gather | solution.py:190
  30.6 84.2 %copy-start.36 = (f32[64]{0:T(128)}, f32[64]{0:T(128)S(1)}, u32[]{:S(2)}) copy-start(f32[64]{0:T(128)S(1)} %broadcast_multiply_fusion.3) | copy-start | bytes 772
  50.5 64.4 %copy-start.37 = (f32[64]{0:T(128)}, f32[64]{0:T(128)S(1)}, u32[]{:S(2)}) copy-start(f32[64]{0:T(128)S(1)} %add_rsqrt_fusion.3) | copy-start | bytes 772
  208.3 70.3 %copy-start.4 = (bf16[1,64,3072]{2,1,0:T(8,128)(2,1)S(1)}, bf16[1,64,3072]{2,1,0:T(8,128)(2,1)}, u32[]{:S(2)}) copy-start(bf16[1,64,3072]{2,1,0:T(8,128)(2,1)} %fusion.63) | copy-start | bytes 1179652
  284.0 54.8 %copy-start.1 = (bf16[1,448,3072]{2,1,0:T(8,128)(2,1)S(1)}, bf16[1,448,3072]{2,1,0:T(8,128)(2,1)}, u32[]{:S(2)}) copy-start(bf16[1,448,3072]{2,1,0:T(8,128)(2,1)} %all-gather.10.cloned.1.call-done) | copy-start | bytes 8257540
  351.0 4.7 copy-start.29
  351.0 4.7 copy-start.30
  354.7 2.9 copy-start.22
  354.7 2.9 copy-start.25
  377.6 4.3 copy-start.16
  384.5 139.8 %reduce-scatter.5.cloned.1.call-start = ((), (), s32[]{:S(2)}) async-start(), calls=%async_computation.8 | async-start | bytes 3932160 | tf_op jit(solution)/shard_map/reduce_scatter | solution.py:116
  399.1 10.1 %copy-start.13 = (bf16[3072,512,1]{1,0,2:T(8,128)(2,1)S(1)}, bf16[3072,512,1]{1,0,2:T(8,128)(2,1)}, u32[]{:S(2)}) copy-start(bf16[3072,512,1]{1,0,2:T(8,128)(2,1)} %reshape.259) | copy-start | bytes 9437188
  414.1 173.9 %reduce-scatter.7.cloned.1.call-start = ((), (), s32[]{:S(2)}) async-start(), calls=%async_computation.11 | async-start | bytes 17694720
  415.1 3.6 copy-start.19
  475.9 24.2 %copy-start.11 = (bf16[64,3,4,128]{0,3,2,1:T(8,128)(2,1)S(1)}, bf16[64,3,4,128]{0,3,2,1:T(8,128)(2,1)}, u32[]{:S(2)}) copy-start(bf16[64,3,4,128]{0,3,2,1:T(8,128)(2,1)} %pad_maximum_fusion.5) | copy-start | bytes 589828
  500.1 7.3 %copy-start.20 = (bf16[448,3,4,128]{0,3,2,1:T(8,128)(2,1)S(1)}, bf16[448,3,4,128]{0,3,2,1:T(8,128)(2,1)}, u32[]{:S(2)}) copy-start(bf16[448,3,4,128]{0,3,2,1:T(8,128)(2,1)} %copy-done.19) | copy-start | bytes 4128772
  500.1 7.4 %copy-start.39 = (f32[448]{0:T(512)S(1)}, f32[448]{0:T(512)}, u32[]{:S(2)}) copy-start(f32[448]{0:T(512)} %add_rsqrt_fusion.2) | copy-start | bytes 5380
  507.4 9.6 %copy-start.18 = (bf16[1,64,8,384]{3,1,2,0:T(8,128)(2,1)S(1)}, bf16[1,64,8,384]{3,1,2,0:T(8,128)(2,1)}, u32[]{:S(2)}) copy-start(bf16[1,64,8,384]{3,1,2,0:T(8,128)(2,1)} %copy.74) | copy-start | bytes 1179652
  522.4 3.2 copy-start.24
  522.4 3.9 copy-start.14
  522.4 3.9 copy-start.32
  593.4 3.6 copy-start.3
  (18 other events, 31.4 us)
Sparse Core Ops, SparseCore 0:
  9.6 68.0 all-gather.9
  79.5 31.1 all-gather.13
  112.6 32.1 all-gather.15
  146.3 56.9 all-gather.17
  204.9 57.4 all-gather.7
  264.1 58.6 all-gather.11
  384.6 25.6 all-gather.19
  414.2 60.3 reduce-scatter.4
  478.1 109.8 reduce-scatter.6
where the time goes:
time: 612 us; the launch traced here: 606 us
  waiting for transfers between devices  264 us (43%)
  local copies, waits for them, and re-layouts  126 us (21%)
  matrix products  84.2 us (14%)
  blocking collectives  70.6 us (12%)
  other arithmetic  46.6 us (8%)
  between operations  14.7 us (2%)
    all_gather x1, waiting for transfers between devices, body(): lax.all_gather(text_qkv_weight, 'dp', axis=0, tiled=True)  54.1 us
    unnamed x93, local copies, waits for them, and re-layouts  51.8 us
    all_gather x1, waiting for transfers between devices, body(): lax.all_gather(image_slope, 'context', axis=1, tiled=True)  46.9 us
    unnamed x10, waiting for transfers between devices  43.6 us
    all_gather x1, waiting for transfers between devices, body(): lax.all_gather(image_qkv_weight, 'dp', axis=0, tiled=True)  38.9 us
    all_gather x1, waiting for transfers between devices, body(): lax.all_gather(text_out_weight, 'dp', axis=0, tiled=True)  29 us
    all_gather x1, waiting for transfers between devices, body(): lax.all_gather(image_out_weight, 'dp', axis=0, tiled=True)  26.6 us
    all_gather x1, waiting for transfers between devices, body(): lax.all_gather(image_tokens, 'context', axis=1, tiled=True)  24.9 us
  transfers between devices with their start and end apart: 9, of which 7 were waited for; matrix products, arithmetic and copies ran while one was open for 30% of the time, Pallas kernels for 0%

commit v1 on v0

--- a/solution.py
+++ b/solution.py
@@ -4,6 +4,21 @@
 from jax.sharding import PartitionSpec as P
 
 norm_eps = 1e-06
+
+
+def tasks_search(buf):
+    big = lax.axis_index("dp")
+    u_next = lax.axis_size("dp")
+    shaped, row_out, formed = (u_next, big, buf.shape[0])
+    history = [(dev, (dev + 1) % shaped) for dev in range(shaped)]
+    front = buf
+    back = jnp.zeros((*buf.shape[:0], shaped * formed, *buf.shape[1:]), buf.dtype)
+    for to_i in range(shaped):
+        all_values = (row_out - to_i) % shaped
+        back = lax.dynamic_update_slice_in_dim(back, front, all_values * formed, axis=0)
+        if to_i < shaped - 1:
+            front = lax.ppermute(front, axis_name="dp", perm=history)
+    return back
 
 
 def layer_normal(values):
@@ -71,7 +86,7 @@
     )
     full_q_image, full_q_text, full_o_image, full_o_text = (
         lax.all_gather(image_qkv_weight, "dp", axis=0, tiled=True),
-        lax.all_gather(text_qkv_weight, "dp", axis=0, tiled=True),
+        tasks_search(text_qkv_weight),
         lax.all_gather(image_out_weight, "dp", axis=0, tiled=True),
         lax.all_gather(text_out_weight, "dp", axis=0, tiled=True),
     )

time: 612 us -> 567 us (0.926)
  waiting for transfers between devices: 264 us -> 196 us
  local copies, waits for them, and re-layouts: 126 us -> 142 us
    ppermute x0 -> x7, waiting for transfers between devices: none -> 89.5 us  [tasks_search(): front = lax.ppermute(front, axis_name='dp', perm=history)]
    all_gather x1 -> x0, waiting for transfers between devices: 54.1 us -> none  [body(): lax.all_gather(text_qkv_weight, 'dp', axis=0, tiled=True)]
    all_gather x1, waiting for transfers between devices: 29 us -> 0.01 us  [body(): lax.all_gather(text_out_weight, 'dp', axis=0, tiled=True)]
    all_gather x1, waiting for transfers between devices: 26.6 us -> 0.01 us  [body(): lax.all_gather(image_out_weight, 'dp', axis=0, tiled=True)]
    all_gather x1, waiting for transfers between devices: 24.9 us -> 0.01 us  [body(): lax.all_gather(image_tokens, 'context', axis=1, tiled=True)]
    all_gather x1, waiting for transfers between devices: 38.9 us -> 23.2 us  [body(): lax.all_gather(image_qkv_weight, 'dp', axis=0, tiled=True)]
    dynamic_update_slice x0 -> x8, local copies, waits for them, and re-layouts: none -> 15.4 us  [tasks_search(): lax.dynamic_update_slice_in_dim(back, front, all_values * formed, axis=0)]
    all_gather x1, waiting for transfers between devices: 46.9 us -> 40.3 us  [body(): lax.all_gather(image_slope, 'context', axis=1, tiled=True)]
  transfers between devices with their start and end apart: 9 -> 15, of which waited for: 7 -> 8; matrix products, arithmetic and copies ran while one was open for 30% -> 36% of each run, Pallas kernels for 0% -> 0%
where the time goes in v1:
time: 567 us; the launch traced here: 560 us
  waiting for transfers between devices  196 us (35%)
  local copies, waits for them, and re-layouts  142 us (25%)
  matrix products  84.7 us (15%)
  blocking collectives  72 us (13%)
  other arithmetic  48.1 us (8%)
  between operations  15 us (3%)
    ppermute x7, waiting for transfers between devices, tasks_search(): front = lax.ppermute(front, axis_name='dp', perm=history)  89.5 us
    unnamed x95, local copies, waits for them, and re-layouts  51.2 us
    unnamed x9, waiting for transfers between devices  43 us
    all_gather x1, waiting for transfers between devices, body(): lax.all_gather(image_slope, 'context', axis=1, tiled=True)  40.3 us
    all_gather x1, waiting for transfers between devices, body(): lax.all_gather(image_qkv_weight, 'dp', axis=0, tiled=True)  23.2 us
    dot_general x4, matrix products, contract_last(): lax.dot_general(left_side, right_side, (((1,), (1,)), ((), ())), preferre...  22.8 us
    all_gather x1, blocking collectives, body(): lax.all_gather(text_tokens, 'context', axis=1, tiled=True)  21 us
    psum x1, blocking collectives, body(): lax.psum(part_image.astype(jnp.bfloat16), 'context').astype(jnp.float32)  19.3 us
  transfers between devices with their start and end apart: 15, of which 8 were waited for; matrix products, arithmetic and copies ran while one was open for 36% of the time, Pallas kernels for 0%

profile of v1, /device:TPU:0, one launch (start us, length us, event | category | flops | bytes accessed | tf_op | source)
XLA Modules:
  0.0 559.7 jit_solution(870199572671521147)
XLA Ops:
  11.1 17.0 %collective-permute-done = bf16[384,3,4,128]{3,2,1,0:T(4,128)(2,1)S(1)} collective-permute-done((bf16[384,3,4,128]{3,2,1,0:T(4,128)(2,1)}, bf16[384,3,4,128]{3,2,1,0:T(4,128)(2,1)S(1)}, u32[]{:S(2)}, u32[]{:S(2)}) %collective-permute-start) | collective-permute-done | bytes 1179680 | tf_op jit(solution)/shard_map/ppermute | solution.py:20
  29.6 21.0 %all_gather.24 = bf16[1,64,3072]{2,1,0:T(8,128)(2,1)S(1)} all-gather(bf16[1,16,3072]{2,1,0:T(8,128)(2,1)} %param.11), channel_id=1, replica_groups=mesh['dp'=8,'context'=4] {'context'}, dimensions={1}, use_global_device_ids=true | all-gather | bytes 491520 | tf_op jit(solution)/shard_map/all_gather | solution.py:83
  50.8 4.1 broadcast_in_dim.18
  56.3 19.1 %all_gather.29 = bf16[1,64,3072]{2,1,0:T(8,128)(2,1)} all-gather(bf16[1,16,3072]{2,1,0:T(8,128)(2,1)S(1)} %copy-done.25), channel_id=1, replica_groups=mesh['dp'=8,'context'=4] {'context'}, dimensions={1}, use_global_device_ids=true | all-gather | bytes 491520 | tf_op jit(solution)/shard_map/all_gather | solution.py:85
  75.5 16.5 %collective-permute-done.2 = bf16[384,3,4,128]{3,2,1,0:T(4,128)(2,1)S(1)} collective-permute-done((bf16[384,3,4,128]{3,2,1,0:T(4,128)(2,1)S(1)}, bf16[384,3,4,128]{3,2,1,0:T(4,128)(2,1)S(1)}, u32[]{:S(2)}, u32[]{:S(2)}) %collective-permute-start.2) | collective-permute-done | bytes 1179680 | tf_op jit(solution)/shard_map/ppermute | solution.py:20
  93.2 23.0 %collective-permute-done.3 = bf16[384,3,4,128]{3,2,1,0:T(4,128)(2,1)S(1)} collective-permute-done((bf16[384,3,4,128]{3,2,1,0:T(4,128)(2,1)S(1)}, bf16[384,3,4,128]{3,2,1,0:T(4,128)(2,1)S(1)}, u32[]{:S(2)}, u32[]{:S(2)}) %collective-permute-start.3) | collective-permute-done | bytes 1179680 | tf_op jit(solution)/shard_map/ppermute | solution.py:20
  118.9 14.8 %collective-permute-done.4 = bf16[384,3,4,128]{3,2,1,0:T(4,128)(2,1)} collective-permute-done((bf16[384,3,4,128]{3,2,1,0:T(4,128)(2,1)S(1)}, bf16[384,3,4,128]{3,2,1,0:T(4,128)(2,1)}, u32[]{:S(2)}, u32[]{:S(2)}) %collective-permute-start.4) | collective-permute-done | bytes 1179680 | tf_op jit(solution)/shard_map/ppermute | solution.py:20
  140.6 18.4 %collective-permute-done.5 = bf16[384,3,4,128]{3,2,1,0:T(4,128)(2,1)} collective-permute-done((bf16[384,3,4,128]{3,2,1,0:T(4,128)(2,1)}, bf16[384,3,4,128]{3,2,1,0:T(4,128)(2,1)}, u32[]{:S(2)}, u32[]{:S(2)}) %collective-permute-start.5) | collective-permute-done | bytes 1179680 | tf_op jit(solution)/shard_map/ppermute | solution.py:20
  166.1 4.5 copy.103
  176.4 40.3 %all-gather.15.cloned.1.call-done = bf16[1,448,3072]{2,1,0:T(8,128)(2,1)} async-done(((bf16[1,112,3072]{2,1,0:T(8,128)(2,1)}), bf16[1,448,3072]{2,1,0:T(8,128)(2,1)}) %all-gather.15.cloned.1.call-update) | async-done | bytes 2752528 | tf_op jit(solution)/shard_map/all_gather | solution.py:84
  216.7 5.1 fusion.49
  230.1 16.0 %reshape.247 = bf16[3072,1536]{1,0:T(8,128)(2,1)} reshape(bf16[3072,3,4,128]{3,2,1,0:T(4,128)(2,1)} %constant_dynamic-update-slice_fusion) | data formatting | bytes 18874368 | tf_op jit(solution)/shard_map/reshape | solution.py:94
  246.1 6.6 %fusion.78 = f32[64,1536]{1,0:T(8,128)S(1)} fusion(bf16[3072,1536]{1,0:T(8,128)(2,1)} %reshape.247, bf16[1,64,3072]{2,1,0:T(8,128)(2,1)S(1)} %copy-done.3), kind=kOutput, calls=%fused_computation.104 | convolution fusion | flops 603979776 | bytes 10223616 | tf_op jit(solution)/shard_map/dot_general | solution.py:101
  252.7 23.2 %all-gather.9.cloned.1.call-done = bf16[3072,3,4,128]{3,2,1,0:T(4,128)(2,1)} async-done(((bf16[384,3,4,128]{3,2,1,0:T(4,128)(2,1)}), bf16[3072,3,4,128]{3,2,1,0:T(4,128)(2,1)}) %all-gather.9.cloned.1.call-update) | async-done | bytes 9437200 | tf_op jit(solution)/shard_map/all_gather | solution.py:88
  275.9 15.9 %reshape.248 = bf16[3072,1536]{1,0:T(8,128)(2,1)} reshape(bf16[3072,3,4,128]{3,2,1,0:T(4,128)(2,1)} %all-gather.9.cloned.1.call-done) | data formatting | bytes 18874368 | tf_op jit(solution)/shard_map/reshape | solution.py:93
  291.8 7.6 %fusion.21 = f32[448,1536]{1,0:T(8,128)S(1)} fusion(bf16[3072,1536]{1,0:T(8,128)(2,1)} %reshape.248, bf16[1,448,3072]{2,1,0:T(8,128)(2,1)S(1)} %copy-done.1, f32[3072]{0:T(1024)} %bitcast.215, f32[448]{0:T(512)} %add_rsqrt_fusion.2, f32[448]{0:T(512)S(1)} %broadcast_multiply_fusion.2, f32[3072]{0:T(1024)} %bitcast.213), kind=kOutput, calls=%fused_computation.37 | convolution fusion | flops 4236115968 | bytes 14970368 | tf_op jit(solution)/shard_map/dot_general | solution.py:102
  313.2 8.0 %fusion.46 = f32[512,4,128]{0,2,1:T(8,128)} fusion(f32[4,512,512]{1,2,0:T(8,128)} %fusion.80, f32[512,3,4,128]{0,3,2,1:T(8,128)S(1)} %bitcast.182, f32[512,4]{0,1:T(4,128)} %copy-done.31, f32[4,512,512]{1,2,0:T(8,128)} %copy-done.9, f32[4,512]{1,0:T(4,128)} %copy-done.36), kind=kOutput, calls=%fused_computation.58 | convolution fusion | flops 278399488 | bytes 18898944 | tf_op jit(solution)/shard_map/hij,ihe->jhe/dot_general | solution.py:165
  321.2 10.0 %multiply_reduce_fusion.2 = (f32[512,4]{0,1:T(4,128)}, f32[512,4]{0,1:T(4,128)}, f32[512,4,128]{0,2,1:T(8,128)}) fusion(f32[512,3,4,128]{0,3,2,1:T(8,128)S(1)} %bitcast.183, f32[512,4]{0,1:T(4,128)} %copy-done.31, f32[512,4,128]{0,2,1:T(8,128)} %fusion.46, f32[512,4]{0,1:T(4,128)} %copy-done.30, f32[4,512,512]{1,2,0:T(8,128)} %fusion.80, ...), kind=kOutput, calls=%fused_computation.74 | convolution fusion | flops 279968256 | bytes 22077440 | tf_op jit(solution)/shard_map/hij,jhe->ihe/dot_general | solution.py:164
  338.2 5.7 %reshape.258 = bf16[3072,512,1]{1,0,2:T(8,128)(2,1)} reshape(bf16[3072,4,128]{2,1,0:T(4,128)(2,1)} %all-gather.11.cloned.1.call-done) | data formatting | bytes 6291456 | tf_op jit(solution)/shard_map/reshape | solution.py:96
  343.9 5.8 %reshape.259 = bf16[3072,512,1]{1,0,2:T(8,128)(2,1)} reshape(bf16[3072,4,128]{2,1,0:T(4,128)(2,1)} %all-gather.13.cloned.1.call-done) | data formatting | bytes 6291456 | tf_op jit(solution)/shard_map/reshape | solution.py:95
  372.8 5.7 %convolution_convert_fusion = bf16[3072,1536]{0,1:T(8,128)(2,1)S(1)} fusion(bf16[448,1536]{0,1:T(8,128)(2,1)S(1)} %bitcast.202, bf16[1,448,3072]{2,1,0:T(8,128)(2,1)S(1)} %copy-done.2, f32[3072]{0:T(1024)S(1)} %bitcast.216, f32[448]{0:T(512)S(1)} %copy-done.39, f32[3072]{0:T(1024)S(1)} %bitcast.214, f32[448]{0:T(512)S(1)} %broadcast_multiply_fusion.2), kind=kOutput, calls=%fused_computation.3 | convolution fusion | flops 4240834560 | bytes 13594112 | tf_op jit(solution)/shard_map/dot_general | solution.py:46
  378.6 7.7 %pad_maximum_fusion = bf16[3072,2560]{0,1:T(8,128)(2,1)} fusion(bf16[3072,512]{0,1:T(8,128)(2,1)S(1)} %convolution_convert_fusion.2, bf16[3072,512]{0,1:T(8,128)(2,1)S(1)} %convolution_convert_fusion.3, bf16[3072,1536]{0,1:T(8,128)(2,1)S(1)} %convolution_convert_fusion), kind=kLoop, calls=%fused_computation.2 | loop fusion | flops 47185920 | bytes 31457280 | tf_op jit(solution)/shard_map/concatenate | solution.py:200
  386.2 19.7 %copy.92 = bf16[3072,2560]{1,0:T(8,128)(2,1)} copy(bf16[3072,2560]{0,1:T(8,128)(2,1)} %pad_maximum_fusion) | data formatting | bytes 31457280
  410.4 18.9 %reduce.2 = bf16[3072,64]{1,0:T(8,128)(2,1)} reduce(bf16[3072,1,64]{2,1,0:T(2,128)(2,1)} %bitcast.193, bf16[]{:T(256)} %broadcast.217), dimensions={1}, to_apply=%bitcast.152.reduce_sub_computation | reduce | bytes 786434
  432.0 12.6 %all_to_all.18 = bf16[8,2,12288]{2,1,0:T(2,128)(2,1)} all-to-all(bf16[8,2,12288]{2,1,0:T(2,128)(2,1)} %reshape.268), channel_id=1, replica_groups=mesh['dp'=8,'context'=4] {'dp'}, dimensions={0} | all-to-all | bytes 786432 | tf_op jit(solution)/shard_map/all_to_all | solution.py:204
  444.6 3.8 reshape.269
  453.6 7.3 %fusion.103 = (bf16[3072]{0:T(1024)(128)(2,1)S(1)}, bf16[3072]{0:T(1024)(128)(2,1)S(1)}) fusion(f32[64]{0:T(128)} %copy-done.38, f32[64]{0:T(128)} %copy-done.37, bf16[1,64,3072]{2,1,0:T(8,128)(2,1)S(1)} %all_gather.24, bf16[64,1536]{0,1:T(8,128)(2,1)S(1)} %bitcast.196, bf16[3072,1536]{1,0:T(8,128)(2,1)} %reshape.247), kind=kOutput, calls=%fused_computation.139 | convolution fusion | flops 605153280 | bytes 10039808 | tf_op jit(solution)/shard_map/dot_general | solution.py:52
  461.0 9.5 %fusion.102 = (bf16[3072]{0:T(1024)(128)(2,1)S(1)}, bf16[3072]{0:T(1024)(128)(2,1)S(1)}) fusion(f32[448]{0:T(512)S(1)} %copy-done.40, f32[448]{0:T(512)S(1)} %broadcast_multiply_fusion.2, bf16[1,448,3072]{2,1,0:T(8,128)(2,1)S(1)} %copy-done.2, bf16[448,1536]{0,1:T(8,128)(2,1)S(1)} %bitcast.203, bf16[3072,1536]{1,0:T(8,128)(2,1)} %reshape.248), kind=kOutput, calls=%fused_computation.138 | convolution fusion | flops 4236109824 | bytes 13581824 | tf_op jit(solution)/shard_map/dot_general | solution.py:52
  470.5 4.0 convolution_convert_fusion.1
  481.1 19.3 %all-reduce = (bf16[1,3,3072]{2,0,1:T(2,128)(2,1)S(1)}, bf16[1,3,3072]{2,0,1:T(2,128)(2,1)S(1)}) all-reduce(bf16[1,3,3072]{2,0,1:T(2,128)(2,1)S(1)} %broadcast_in_dim.41, bf16[1,3,3072]{2,0,1:T(2,128)(2,1)S(1)} %broadcast_in_dim.43), channel_id=1, replica_groups=mesh['dp'=8,'context'=4] {'context'}, use_global_device_ids=true, to_apply=%region_16.17 | all-reduce | flops 18432 | bytes 73728 | tf_op jit(solution)/shard_map/psum | solution.py:193
  501.7 39.8 %reduce-scatter.7.cloned.1.call-done = bf16[384,2560]{1,0:T(8,128)(2,1)} async-done(((bf16[3072,2560]{1,0:T(8,128)(2,1)}), bf16[384,2560]{1,0:T(8,128)(2,1)}) %reduce-scatter.7.cloned.1.call-update) | async-done | bytes 1966096
  546.1 4.3 copy.76
  (193 shorter events, 109.8 us)
Async XLA Ops:
  7.2 129.4 %all-gather.7.cloned.1.call-start = ((), (), s32[]{:S(2)}) async-start(), calls=%async_computation.3 | async-start | bytes 3440640 | tf_op jit(solution)/shard_map/all_gather | solution.py:82
  7.9 152.6 %all-gather.13.cloned.1.call-start = ((), (), s32[]{:S(2)}) async-start(), calls=%async_computation.6 | async-start | bytes 3538944 | tf_op jit(solution)/shard_map/all_gather | solution.py:90
  8.6 157.4 %all-gather.11.cloned.1.call-start = ((), (), s32[]{:S(2)}) async-start(), calls=%async_computation.5 | async-start | bytes 3538944 | tf_op jit(solution)/shard_map/all_gather | solution.py:91
  9.4 207.3 %all-gather.15.cloned.1.call-start = ((), (), s32[]{:S(2)}) async-start(), calls=%async_computation.8 | async-start | bytes 3440640 | tf_op jit(solution)/shard_map/all_gather | solution.py:84
  10.0 265.9 %all-gather.9.cloned.1.call-start = ((), (), s32[]{:S(2)}) async-start(), calls=%async_computation.4 | async-start | bytes 10616832 | tf_op jit(solution)/shard_map/all_gather | solution.py:88
  10.5 460.0 %all-gather.17.cloned.1.call-start = ((), (), s32[]{:S(2)}) async-start(), calls=%async_computation.9 | async-start | bytes 1769472 | tf_op jit(solution)/shard_map/all_gather | solution.py:205
  10.6 17.5 %collective-permute-start = (bf16[384,3,4,128]{3,2,1,0:T(4,128)(2,1)}, bf16[384,3,4,128]{3,2,1,0:T(4,128)(2,1)S(1)}, u32[]{:S(2)}, u32[]{:S(2)}) collective-permute-start(bf16[384,3,4,128]{3,2,1,0:T(4,128)(2,1)} %param.15), channel_id=1, source_target_pairs={{0,4},{4,8},{8,12},{12,16},{16,20},{20,24},{24,28},{28,0},{1,5},{5... | collective-permute-start | bytes 3538952 | tf_op jit(solution)/shard_map/ppermute | solution.py:20
  28.1 47.3 %collective-permute-start.1 = (bf16[384,3,4,128]{3,2,1,0:T(4,128)(2,1)S(1)}, bf16[384,3,4,128]{3,2,1,0:T(4,128)(2,1)S(1)}, u32[]{:S(2)}, u32[]{:S(2)}) collective-permute-start(bf16[384,3,4,128]{3,2,1,0:T(4,128)(2,1)S(1)} %collective-permute-done), channel_id=1, source_target_pairs={{0,4},{4,8},{8,12},{12,16},{16,20},{20,24},{24,28},{28,0},{1,5},{5... | collective-permute-start | bytes 3538952 | tf_op jit(solution)/shard_map/ppermute | solution.py:20
  50.7 4.1 copy-start.20
  50.7 5.6 copy-start.25
  50.8 24.7 %copy-start.28 = (bf16[1,3,3072]{2,1,0:T(4,128)(2,1)S(1)}, bf16[1,3,3072]{2,1,0:T(4,128)(2,1)}, u32[]{:S(2)}) copy-start(bf16[1,3,3072]{2,1,0:T(4,128)(2,1)} %param.13) | copy-start | bytes 55300
  50.8 41.2 %copy-start.29 = (bf16[1,3,3072]{2,1,0:T(4,128)(2,1)S(1)}, bf16[1,3,3072]{2,1,0:T(4,128)(2,1)}, u32[]{:S(2)}) copy-start(bf16[1,3,3072]{2,1,0:T(4,128)(2,1)} %param.12) | copy-start | bytes 55300
  75.4 61.1 %copy-start.37 = (f32[64]{0:T(128)}, f32[64]{0:T(128)S(1)}, u32[]{:S(2)}) copy-start(f32[64]{0:T(128)S(1)} %broadcast_multiply_fusion.3) | copy-start | bytes 772
  75.4 16.6 %collective-permute-start.2 = (bf16[384,3,4,128]{3,2,1,0:T(4,128)(2,1)S(1)}, bf16[384,3,4,128]{3,2,1,0:T(4,128)(2,1)S(1)}, u32[]{:S(2)}, u32[]{:S(2)}) collective-permute-start(bf16[384,3,4,128]{3,2,1,0:T(4,128)(2,1)S(1)} %collective-permute-done.1), channel_id=1, source_target_pairs={{0,4},{4,8},{8,12},{12,16},{16,20},{20,24},{24,28},{28,0},{1,5},{5... | collective-permute-start | bytes 3538952 | tf_op jit(solution)/shard_map/ppermute | solution.py:20
  92.0 24.2 %collective-permute-start.3 = (bf16[384,3,4,128]{3,2,1,0:T(4,128)(2,1)S(1)}, bf16[384,3,4,128]{3,2,1,0:T(4,128)(2,1)S(1)}, u32[]{:S(2)}, u32[]{:S(2)}) collective-permute-start(bf16[384,3,4,128]{3,2,1,0:T(4,128)(2,1)S(1)} %collective-permute-done.2), channel_id=1, source_target_pairs={{0,4},{4,8},{8,12},{12,16},{16,20},{20,24},{24,28},{28,0},{1,5},{5... | collective-permute-start | bytes 3538952 | tf_op jit(solution)/shard_map/ppermute | solution.py:20
  116.2 18.9 %copy-start.21 = (bf16[384,3,4,128]{3,2,1,0:T(4,128)(2,1)}, bf16[384,3,4,128]{3,2,1,0:T(4,128)(2,1)S(1)}, u32[]{:S(2)}) copy-start(bf16[384,3,4,128]{3,2,1,0:T(4,128)(2,1)S(1)} %collective-permute-done.3) | copy-start | bytes 3538948
  116.2 17.5 %collective-permute-start.4 = (bf16[384,3,4,128]{3,2,1,0:T(4,128)(2,1)S(1)}, bf16[384,3,4,128]{3,2,1,0:T(4,128)(2,1)}, u32[]{:S(2)}, u32[]{:S(2)}) collective-permute-start(bf16[384,3,4,128]{3,2,1,0:T(4,128)(2,1)S(1)} %collective-permute-done.3), channel_id=1, source_target_pairs={{0,4},{4,8},{8,12},{12,16},{16,20},{20,24},{24,28},{28,0},{1,5},{5... | collective-permute-start | bytes 3538952 | tf_op jit(solution)/shard_map/ppermute | solution.py:20
  116.5 22.4 %copy-start.38 = (f32[64]{0:T(128)}, f32[64]{0:T(128)S(1)}, u32[]{:S(2)}) copy-start(f32[64]{0:T(128)S(1)} %add_rsqrt_fusion.3) | copy-start | bytes 772
  133.7 25.3 %collective-permute-start.5 = (bf16[384,3,4,128]{3,2,1,0:T(4,128)(2,1)}, bf16[384,3,4,128]{3,2,1,0:T(4,128)(2,1)}, u32[]{:S(2)}, u32[]{:S(2)}) collective-permute-start(bf16[384,3,4,128]{3,2,1,0:T(4,128)(2,1)} %collective-permute-done.4), channel_id=1, source_target_pairs={{0,4},{4,8},{8,12},{12,16},{16,20},{20,24},{24,28},{28,0},{1,5},{5... | collective-permute-start | bytes 3538952 | tf_op jit(solution)/shard_map/ppermute | solution.py:20
  136.5 22.6 %copy-start.22 = (bf16[384,3,4,128]{3,2,1,0:T(4,128)(2,1)S(1)}, bf16[384,3,4,128]{3,2,1,0:T(4,128)(2,1)}, u32[]{:S(2)}) copy-start(bf16[384,3,4,128]{3,2,1,0:T(4,128)(2,1)} %copy-done.21) | copy-start | bytes 3538948
  158.9 68.5 %collective-permute-start.6 = (bf16[384,3,4,128]{3,2,1,0:T(4,128)(2,1)}, bf16[384,3,4,128]{3,2,1,0:T(4,128)(2,1)}, u32[]{:S(2)}, u32[]{:S(2)}) collective-permute-start(bf16[384,3,4,128]{3,2,1,0:T(4,128)(2,1)} %collective-permute-done.5), channel_id=1, source_target_pairs={{0,4},{4,8},{8,12},{12,16},{16,20},{20,24},{24,28},{28,0},{1,5},{5... | collective-permute-start | bytes 3538952 | tf_op jit(solution)/shard_map/ppermute | solution.py:20
  230.1 16.0 %copy-start.3 = (bf16[1,64,3072]{2,1,0:T(8,128)(2,1)S(1)}, bf16[1,64,3072]{2,1,0:T(8,128)(2,1)}, u32[]{:S(2)}) copy-start(bf16[1,64,3072]{2,1,0:T(8,128)(2,1)} %fusion.63) | copy-start | bytes 1179652
  252.7 39.1 %copy-start.1 = (bf16[1,448,3072]{2,1,0:T(8,128)(2,1)S(1)}, bf16[1,448,3072]{2,1,0:T(8,128)(2,1)}, u32[]{:S(2)}) copy-start(bf16[1,448,3072]{2,1,0:T(8,128)(2,1)} %all-gather.7.cloned.1.call-done) | copy-start | bytes 8257540
  331.2 4.3 copy-start.15
  338.1 139.7 %reduce-scatter.5.cloned.1.call-start = ((), (), s32[]{:S(2)}) async-start(), calls=%async_computation.7 | async-start | bytes 3932160 | tf_op jit(solution)/shard_map/reduce_scatter | solution.py:131
  352.7 10.1 %copy-start.12 = (bf16[3072,512,1]{1,0,2:T(8,128)(2,1)S(1)}, bf16[3072,512,1]{1,0,2:T(8,128)(2,1)}, u32[]{:S(2)}) copy-start(bf16[3072,512,1]{1,0,2:T(8,128)(2,1)} %reshape.259) | copy-start | bytes 9437188
  367.7 173.9 %reduce-scatter.7.cloned.1.call-start = ((), (), s32[]{:S(2)}) async-start(), calls=%async_computation.10 | async-start | bytes 17694720
  429.2 24.4 %copy-start.10 = (bf16[64,3,4,128]{0,3,2,1:T(8,128)(2,1)S(1)}, bf16[64,3,4,128]{0,3,2,1:T(8,128)(2,1)}, u32[]{:S(2)}) copy-start(bf16[64,3,4,128]{0,3,2,1:T(8,128)(2,1)} %pad_maximum_fusion.5) | copy-start | bytes 589828
  453.6 7.4 %copy-start.19 = (bf16[448,3,4,128]{0,3,2,1:T(8,128)(2,1)S(1)}, bf16[448,3,4,128]{0,3,2,1:T(8,128)(2,1)}, u32[]{:S(2)}) copy-start(bf16[448,3,4,128]{0,3,2,1:T(8,128)(2,1)} %copy-done.18) | copy-start | bytes 4128772
  453.6 7.4 %copy-start.40 = (f32[448]{0:T(512)S(1)}, f32[448]{0:T(512)}, u32[]{:S(2)}) copy-start(f32[448]{0:T(512)} %add_rsqrt_fusion.2) | copy-start | bytes 5380
  461.0 9.5 %copy-start.17 = (bf16[1,64,8,384]{3,1,2,0:T(8,128)(2,1)S(1)}, bf16[1,64,8,384]{3,1,2,0:T(8,128)(2,1)}, u32[]{:S(2)}) copy-start(bf16[1,64,8,384]{3,1,2,0:T(8,128)(2,1)} %copy.74) | copy-start | bytes 1179652
  475.9 4.0 copy-start.13
  (25 other events, 53.6 us)
Sparse Core Ops, SparseCore 0:
  9.5 72.0 all-gather.6
  83.5 36.6 all-gather.12
  122.1 37.1 all-gather.10
  160.7 56.0 all-gather.14
  218.4 57.4 all-gather.8
  338.2 25.6 all-gather.16
  367.8 60.3 reduce-scatter.4
  431.7 109.8 reduce-scatter.6
